TPU v7x, 256 devices: a whole 4x4x8 slice. The times are simulated.
256 devices in a mesh: blk: 64 (over x, z, y_hi), col: 4 (over y_lo, core).
Axes of the slice: x: 4, y: 4 (y_hi: 2, y_lo: 2; y = y_hi * 2 + y_lo), z: 8, core: 2. Of those that a mesh axis runs over, the one named last changes fastest.
Arguments:
- points: bfloat16 [32768, 128], P(('blk', 'col')), may hold values from -4.5 to 4.5
- targets: float32 [32768, 32], P(('blk', 'col')), may hold values from -6 to 6
- pivots: int32 [2, 256], replicated, may hold values from 0 to 32767, as said below
Outputs:
- factor: bfloat16 [32768, 512], P(('blk', 'col'))
- solution: float32 [32768, 32], P(('blk', 'col'))
- residual: float32 [32768, 32], P(('blk', 'col'))
Inputs may be any that keep to these rules, and one draw needn't show every extreme that they name: `pivots`: the 512 indices are distinct; 0 and 32767 are among them.
All inputs are finite; a program needn't handle non-finite values.
Results may differ from a plain program's by a relative error of at most 0.012.
Values may be sent and summed in bfloat16 or wider, within the bound.
No kernel may reach another device: no remote copies, remote signals or barrier semaphores. Data moves between devices by JAX's collectives and lax.ppermute only.
A program may use at most 64 MiB of HBM per device.

v0:
```python
import jax
import jax.numpy as jnp
from jax import lax
from jax.sharding import PartitionSpec as P

FEATURES = 128
ITERS = 3
noise_level = 0.5
jitter_level = 0.05
highest = lax.Precision.HIGHEST


def squared_norms(point_rows):
    wide_rows = point_rows.astype(jnp.float32)
    return jnp.sum(wide_rows * wide_rows, axis=1)


def kernel_block(left_rows, left_norms, right_rows, right_norms):
    inner = lax.dot_general(
        left_rows, right_rows, (((1,), (1,)), ((), ())), preferred_element_type=jnp.float32
    )
    distance = left_norms[:, None] + right_norms[None, :] - 2.0 * inner
    return jnp.exp(-2.0 * distance / FEATURES)


def lower_solve(lower_factor, right_rows):
    return jax.scipy.linalg.solve_triangular(lower_factor, right_rows.T, lower=True).T


def build_factor(point_rows, first_pick, second_pick):
    row_norms = squared_norms(point_rows)
    first_norms = squared_norms(first_pick)
    second_norms = squared_norms(second_pick)
    identity_piv = jnp.eye(first_pick.shape[0], dtype=jnp.float32)
    first_chol = jnp.linalg.cholesky(
        kernel_block(first_pick, first_norms, first_pick, first_norms) + jitter_level * identity_piv
    )
    first_coef = lower_solve(
        first_chol, kernel_block(point_rows, row_norms, first_pick, first_norms)
    )
    shared_coef = lower_solve(
        first_chol, kernel_block(second_pick, second_norms, first_pick, first_norms)
    )
    schur_block = (
        kernel_block(second_pick, second_norms, second_pick, second_norms)
        + jitter_level * identity_piv
        - jnp.dot(shared_coef, shared_coef.T, precision=highest)
    )
    second_chol = jnp.linalg.cholesky(schur_block)
    second_cross = kernel_block(point_rows, row_norms, second_pick, second_norms) - jnp.dot(
        first_coef, shared_coef.T, precision=highest
    )
    second_coef = lower_solve(second_chol, second_cross)
    return jnp.concatenate([first_coef, second_coef], axis=1)


def per_device(points, targets, pivots):
    row_count = points.shape[0]
    piv_count = pivots.shape[1]
    shard_index = lax.axis_index("blk") * lax.axis_size("col") + lax.axis_index("col")
    first_row = shard_index * row_count
    flat_pivots = pivots.reshape(-1)
    owned = (
        flat_pivots[:, None] == first_row + jnp.arange(row_count, dtype=jnp.int32)[None, :]
    ).astype(jnp.float32)
    local_pick = jnp.dot(owned, points.astype(jnp.float32), precision=highest)
    picked = lax.psum(local_pick, ("blk", "col")).astype(jnp.bfloat16)
    wide_factor = build_factor(points, picked[:piv_count], picked[piv_count:])
    factor = wide_factor.astype(jnp.bfloat16)
    local_gram = lax.dot_general(
        wide_factor, wide_factor, (((0,), (0,)), ((), ())), precision=highest
    )
    gram = lax.psum(local_gram, ("blk", "col"))
    gram = gram + noise_level * jnp.eye(2 * piv_count, dtype=jnp.float32)
    gram_chol = jnp.linalg.cholesky(gram)

    def precondition(residual_now):
        local_proj = lax.dot_general(
            wide_factor, residual_now, (((0,), (0,)), ((), ())), precision=highest
        )
        projection = lax.psum(local_proj, ("blk", "col"))
        coefficients = jax.scipy.linalg.cho_solve((gram_chol, True), projection)
        scaled = (
            residual_now - jnp.dot(wide_factor, coefficients, precision=highest)
        ) / noise_level
        return (scaled, lax.psum(jnp.sum(residual_now * scaled, axis=0), ("blk", "col")))

    own_block = lax.all_gather(points, "col", axis=0, tiled=True)
    own_norms = squared_norms(own_block)

    def tile_add(total, key_rows, key_norms, direction_rows):
        weights = kernel_block(own_block, own_norms, key_rows, key_norms)
        return total + jnp.dot(weights, direction_rows, precision=highest)

    solution = jnp.zeros_like(targets)
    residual = targets
    direction_now, inner_now = precondition(residual)
    for step_index in range(ITERS):
        empty = jnp.zeros((own_block.shape[0], direction_now.shape[1]), jnp.float32)
        add_key_rows = lax.all_gather(points.astype(jnp.float32), "blk", axis=0, tiled=True).astype(
            jnp.bfloat16
        )
        fold_direction_rows = lax.all_gather(direction_now, "blk", axis=0, tiled=True)
        piece_rows = add_key_rows.shape[0]
        splits = piece_rows // row_count

        def scan_step(carry, operands):
            return (tile_add(carry, operands[0], operands[1], operands[2]), None)

        stacked = (
            add_key_rows.reshape(splits, row_count, add_key_rows.shape[1]),
            squared_norms(add_key_rows).reshape(splits, row_count),
            fold_direction_rows.reshape(splits, row_count, fold_direction_rows.shape[1]),
        )
        result, unused = lax.scan(scan_step, empty, stacked)
        image = (
            lax.psum_scatter(result, "col", scatter_dimension=0, tiled=True)
            + noise_level * direction_now
        )
        curvature = lax.psum(jnp.sum(direction_now * image, axis=0), ("blk", "col"))
        step_size = inner_now / curvature
        solution = solution + step_size * direction_now
        residual = residual - step_size * image
        if step_index + 1 < ITERS:
            scaled, inner_next = precondition(residual)
            direction_now = scaled + inner_next / inner_now * direction_now
            inner_now = inner_next
    return (factor, solution, residual)


def solution(mesh):
    return jax.shard_map(
        per_device,
        mesh=mesh,
        in_specs=(P(("blk", "col"), None), P(("blk", "col"), None), P()),
        out_specs=(P(("blk", "col"), None), P(("blk", "col"), None), P(("blk", "col"), None)),
        check_vma=False,
    )
```

profile of v0, /device:TPU:1, one launch (start us, length us, event | category | flops | bytes accessed | tf_op | source)
XLA Modules:
  0.0 2410.5 jit_solution(17141482593332180947)
XLA Ops:
  8.9 82.6 %all-reduce.14 = bf16[512,128]{1,0:T(8,128)(2,1)S(1)} all-reduce(f32[512,128]{1,0:T(8,128)S(1)} %fusion.57), channel_id=1, replica_groups=mesh['blk'=64,'col'=4] {'blk','col'}, use_global_device_ids=true, to_apply=%region_0.0 | all-reduce | flops 65536 | bytes 393216 | tf_op jit(solution)/shard_map/psum | solution.py:67
  92.1 11.7 cholesky.354
  103.9 9.8 custom-call.54
  114.3 11.7 cholesky.364
  129.2 4.4 while.53
  130.0 1.4 dynamic-slice.27
  132.1 1.4 dynamic-slice.27
  133.6 19.7 custom-call.55
  156.1 11.7 cholesky.381
  167.8 9.8 custom-call.56
  178.1 11.7 cholesky.391
  192.9 4.0 while.54
  193.5 1.4 bitcast_dynamic-update-slice_fusion.7
  195.5 1.4 bitcast_dynamic-update-slice_fusion.7
  196.9 19.7 custom-call.57
  218.0 2.0 fusion.240
  221.1 251.4 %all-reduce.13.cloned.1.call-done = (f32[512,512]{1,0:T(8,128)}, f32[512,32]{0,1:T(8,128)}) async-done(((f32[512,512]{1,0:T(8,128)}, f32[512,32]{0,1:T(8,128)}), (f32[512,512]{1,0:T(8,128)}, f32[512,32]{0,1:T(8,128)})) %all-reduce.13.cloned.1.call-update) | async-done | bytes 1114128 | tf_op jit(solution)/shard_map/psum | solution.py:73
  472.5 1.4 select_add_fusion
  474.5 11.7 cholesky.166
  486.4 9.8 custom-call.42
  496.9 11.7 cholesky.189
  509.9 10.0 custom-call.43
  520.5 11.7 cholesky.292
  533.0 9.8 custom-call.58
  543.4 11.7 cholesky.305
  558.7 10.4 while.55
  559.3 2.0 bitcast_dynamic-update-slice_fusion.8
  561.9 2.0 bitcast_dynamic-update-slice_fusion.8
  564.5 2.0 bitcast_dynamic-update-slice_fusion.8
  567.1 2.0 bitcast_dynamic-update-slice_fusion.8
  569.1 40.1 %custom-call.59 = f32[4,128,128]{1,2,0:T(8,128)S(1)} custom-call(f32[4,128,128]{2,1,0:T(8,128)} %get-tuple-element.393), custom_call_target="InvertDiagBlocksLowerTriangular" | custom-call | tf_op jit(solution)/shard_map/jit(_cho_solve)/triangular_solve | solution.py:82
  614.2 6.7 all_gather.17
  621.0 92.2 %all-gather.7.cloned.1.call-done = f32[8192,32]{0,1:T(8,128)} async-done(((f32[128,32]{0,1:T(8,128)}), f32[8192,32]{0,1:T(8,128)}) %all-gather.7.cloned.1.call-update) | async-done | bytes 1048592 | tf_op jit(solution)/shard_map/all_gather | solution.py:103
  713.2 3.6 copy.29
  716.7 116.0 %all-gather.5.cloned.1.call-done = bf16[8192,128]{1,0:T(8,128)(2,1)} async-done(((bf16[128,128]{1,0:T(8,128)(2,1)}), bf16[8192,128]{1,0:T(8,128)(2,1)}) %all-gather.5.cloned.1.call-update) | async-done | bytes 2097168 | tf_op jit(solution)/shard_map/all_gather | solution.py:100
  832.7 2.7 multiply_reduce_fusion
  835.5 144.7 %while.50 = (s32[]{:T(128)}, f32[512,32]{0,1:T(8,128)S(1)}, f32[512]{0:T(512)S(1)}, f32[64,128]{1,0:T(8,128)S(1)}, bf16[64,128,128]{2,1,0:T(8,128)(2,1)}, /*inde...) while((s32[]{:T(128)}, f32[512,32]{0,1:T(8,128)S(1)}, ...), condition=%wide.region_23.28_spmd.clone, body=%wide.region_22.27_spmd.clone.sunk | while | flops 42237952 | bytes 889451 | solution.py:115
  980.9 20.1 reduce-scatter.4.cloned.1.call-done
  1001.8 77.0 %all-reduce.2 = (f32[32]{0:T(128)S(1)}, f32[32]{0:T(128)S(1)}) all-reduce(f32[32]{0:T(128)S(1)} %get-tuple-element.431, f32[32]{0:T(128)S(1)} %get-tuple-element.430), channel_id=1, replica_groups=mesh['blk'=64,'col'=4] {'blk','col'}, use_global_device_ids=true, to_apply=%region_19.24 | all-reduce | flops 64 | bytes 512 | tf_op jit(solution)/shard_map/psum | solution.py:86
  1079.9 234.4 %all-reduce.9.cloned.1.call-done = f32[512,32]{0,1:T(8,128)} async-done(((f32[512,32]{0,1:T(8,128)}), f32[512,32]{0,1:T(8,128)}) %all-reduce.9.cloned.1.call-update) | async-done | bytes 65552 | tf_op jit(solution)/shard_map/psum | solution.py:81
  1320.8 74.4 %psum.83 = f32[32]{0:T(128)S(1)} all-reduce(f32[32]{0:T(128)S(1)} %get-tuple-element.537), channel_id=1, replica_groups=mesh['blk'=64,'col'=4] {'blk','col'}, use_global_device_ids=true, to_apply=%region_29.34 | all-reduce | flops 32 | bytes 256 | tf_op jit(solution)/shard_map/psum | solution.py:86
  1396.0 95.6 %all-gather.9.cloned.1.call-done = f32[8192,32]{0,1:T(8,128)} async-done(((f32[128,32]{0,1:T(8,128)}), f32[8192,32]{0,1:T(8,128)}) %all-gather.9.cloned.1.call-update) | async-done | bytes 1048592 | tf_op jit(solution)/shard_map/all_gather | solution.py:103
  1491.5 3.6 copy.30
  1495.1 144.7 %while.51 = (s32[]{:T(128)}, f32[512,32]{0,1:T(8,128)S(1)}, f32[512]{0:T(512)S(1)}, f32[64,128]{1,0:T(8,128)S(1)}, bf16[64,128,128]{2,1,0:T(8,128)(2,1)}, /*inde...) while((s32[]{:T(128)}, f32[512,32]{0,1:T(8,128)S(1)}, ...), condition=%wide.region_31.36_spmd.clone, body=%wide.region_30.35_spmd.clone.sunk | while | flops 42237952 | bytes 889451 | solution.py:115
  1507.4 1.2 convolution_add_fusion.7
  1511.9 1.2 convolution_add_fusion.7
  1516.5 1.2 convolution_add_fusion.7
  1525.5 1.2 convolution_add_fusion.7
  1530.0 1.2 convolution_add_fusion.7
  1543.6 1.2 convolution_add_fusion.7
  1548.1 1.2 convolution_add_fusion.7
  1561.7 1.2 convolution_add_fusion.7
  1566.2 1.2 convolution_add_fusion.7
  1575.2 1.2 convolution_add_fusion.7
  1640.5 21.1 reduce-scatter.6.cloned.1.call-done
  1662.4 77.3 %psum.84 = f32[32]{0:T(128)S(1)} all-reduce(f32[32]{0:T(128)S(1)} %multiply_reduce_fusion.7), channel_id=1, replica_groups=mesh['blk'=64,'col'=4] {'blk','col'}, use_global_device_ids=true, to_apply=%region_34.39 | all-reduce | flops 32 | bytes 256 | tf_op jit(solution)/shard_map/psum | solution.py:120
  1741.6 234.4 %all-reduce.11.cloned.1.call-done = f32[512,32]{0,1:T(8,128)} async-done(((f32[512,32]{0,1:T(8,128)}), f32[512,32]{0,1:T(8,128)}) %all-reduce.11.cloned.1.call-update) | async-done | bytes 65552 | tf_op jit(solution)/shard_map/psum | solution.py:81
  1982.4 74.4 %psum.86 = f32[32]{0:T(128)S(1)} all-reduce(f32[32]{0:T(128)S(1)} %get-tuple-element.539), channel_id=1, replica_groups=mesh['blk'=64,'col'=4] {'blk','col'}, use_global_device_ids=true, to_apply=%region_37.42 | all-reduce | flops 32 | bytes 256 | tf_op jit(solution)/shard_map/psum | solution.py:86
  2057.6 95.6 %all-gather.11.cloned.1.call-done = f32[8192,32]{0,1:T(8,128)} async-done(((f32[128,32]{0,1:T(8,128)}), f32[8192,32]{0,1:T(8,128)}) %all-gather.11.cloned.1.call-update) | async-done | bytes 1048592 | tf_op jit(solution)/shard_map/all_gather | solution.py:103
  2153.2 3.6 copy.31
  2156.8 144.7 %while.52 = (s32[]{:T(128)}, f32[512,32]{0,1:T(8,128)S(1)}, f32[512]{0:T(512)S(1)}, f32[64,128]{1,0:T(8,128)S(1)}, bf16[64,128,128]{2,1,0:T(8,128)(2,1)}, /*inde...) while((s32[]{:T(128)}, f32[512,32]{0,1:T(8,128)S(1)}, ...), condition=%wide.region_39.44_spmd.clone, body=%wide.region_38.43_spmd.clone.sunk | while | flops 42237952 | bytes 889451 | solution.py:115
  2302.1 21.1 reduce-scatter.8.cloned.1.call-done
  2324.8 77.0 %psum.87 = f32[32]{0:T(128)S(1)} all-reduce(f32[32]{0:T(128)S(1)} %multiply_reduce_fusion.5), channel_id=1, replica_groups=mesh['blk'=64,'col'=4] {'blk','col'}, use_global_device_ids=true, to_apply=%region_42.47 | all-reduce | flops 32 | bytes 256 | tf_op jit(solution)/shard_map/psum | solution.py:120
  2401.8 1.4 multiply_subtract_fusion
  (767 shorter events, 463.6 us)
Async XLA Ops:
  7.2 119.0 %copy-start.5 = (bf16[128,128]{1,0:T(8,128)(2,1)S(1)}, bf16[128,128]{1,0:T(8,128)(2,1)}, u32[]{:S(2)}) copy-start(bf16[128,128]{1,0:T(8,128)(2,1)} %param.16) | copy-start | bytes 98308
  7.2 465.3 %all-reduce.13.cloned.1.call-start = ((), (), s32[]{:S(2)}) async-start(), calls=%async_computation.12 | async-start | bytes 2228224 | tf_op jit(solution)/shard_map/psum | solution.py:73
  154.5 65.5 %copy-start.8 = (f32[128,32]{0,1:T(8,128)S(1)}, f32[128,32]{0,1:T(8,128)}, u32[]{:S(2)}) copy-start(f32[128,32]{0,1:T(8,128)} %param.17) | copy-start | bytes 49156
  221.1 492.1 %all-gather.7.cloned.1.call-start = ((), (), s32[]{:S(2)}) async-start(), calls=%async_computation.4 | async-start | bytes 1064960 | tf_op jit(solution)/shard_map/all_gather | solution.py:103
  472.5 1.8 copy-start
  474.5 134.7 %copy-start.9 = (f32[512,32]{0,1:T(8,128)S(1)}, f32[512,32]{0,1:T(8,128)}, u32[]{:S(2)}) copy-start(f32[512,32]{0,1:T(8,128)} %get-tuple-element.501) | copy-start | bytes 196612
  496.5 117.6 %copy-start.6 = (bf16[128,128]{1,0:T(8,128)(2,1)S(1)}, bf16[128,128]{1,0:T(8,128)(2,1)}, u32[]{:S(2)}) copy-start(bf16[128,128]{1,0:T(8,128)(2,1)} %param.16) | copy-start | bytes 98308
  613.3 219.4 %all-gather.5.cloned.1.call-start = ((), (), s32[]{:S(2)}) async-start(), calls=%async_computation.3 | async-start | bytes 2129920 | tf_op jit(solution)/shard_map/all_gather | solution.py:100
  614.1 386.8 %reduce-scatter.4.cloned.1.call-start = ((), (), s32[]{:S(2)}) async-start(), calls=%async_computation.5 | async-start | bytes 81920 | tf_op jit(solution)/shard_map/reduce_scatter | solution.py:117
  980.2 0.6 copy-start.1
  980.8 333.5 %all-reduce.9.cloned.1.call-start = ((), (), s32[]{:S(2)}) async-start(), calls=%async_computation.6 | async-start | bytes 131072 | tf_op jit(solution)/shard_map/psum | solution.py:81
  1079.9 411.7 %all-gather.9.cloned.1.call-start = ((), (), s32[]{:S(2)}) async-start(), calls=%async_computation.7 | async-start | bytes 1064960 | tf_op jit(solution)/shard_map/all_gather | solution.py:103
  1395.9 265.7 %reduce-scatter.6.cloned.1.call-start = ((), (), s32[]{:S(2)}) async-start(), calls=%async_computation.8 | async-start | bytes 81920 | tf_op jit(solution)/shard_map/reduce_scatter | solution.py:117
  1396.0 265.6 %copy-start.4 = (f32[128,32]{0,1:T(8,128)S(1)}, f32[128,32]{0,1:T(8,128)}, u32[]{:S(2)}) copy-start(f32[128,32]{0,1:T(8,128)} %multiply_add_fusion.4) | copy-start | bytes 49156
  1639.8 0.6 copy-start.2
  1640.5 335.5 %all-reduce.11.cloned.1.call-start = ((), (), s32[]{:S(2)}) async-start(), calls=%async_computation.9 | async-start | bytes 131072 | tf_op jit(solution)/shard_map/psum | solution.py:81
  1741.5 411.7 %all-gather.11.cloned.1.call-start = ((), (), s32[]{:S(2)}) async-start(), calls=%async_computation.10 | async-start | bytes 1064960 | tf_op jit(solution)/shard_map/all_gather | solution.py:103
  2057.5 265.7 %reduce-scatter.8.cloned.1.call-start = ((), (), s32[]{:S(2)}) async-start(), calls=%async_computation.11 | async-start | bytes 81920 | tf_op jit(solution)/shard_map/reduce_scatter | solution.py:117
  2057.6 265.6 %copy-start.7 = (f32[128,32]{0,1:T(8,128)S(1)}, f32[128,32]{0,1:T(8,128)}, u32[]{:S(2)}) copy-start(f32[128,32]{0,1:T(8,128)} %multiply_add_fusion.2) | copy-start | bytes 49156
  2301.4 0.6 copy-start.3
Sparse Core Ops, SparseCore 0:
  221.2 251.2 all-reduce.12
  613.5 99.6 all-gather.6
  717.3 115.3 all-gather.4
  981.0 19.9 reduce-scatter.3
  1080.0 234.2 all-reduce.8
  1396.0 95.4 all-gather.8
  1640.6 20.9 reduce-scatter.5
  1741.6 234.2 all-reduce.10
  2057.6 95.4 all-gather.10
  2302.2 20.9 reduce-scatter.7
where the time goes:
time: 2440 us; the launch traced here: 2410 us
  waiting for transfers between devices  1180 us (48%)
  blocking collectives  469 us (19%)
  matrix products  455 us (19%)
  other arithmetic  239 us (10%)
  local copies, waits for them, and re-layouts  35.5 us (1%)
    psum x2, waiting for transfers between devices, precondition(): projection = lax.psum(local_proj, ('blk', 'col'))  469 us
    all_gather x3, waiting for transfers between devices, per_device(): lax.all_gather(direction_now, 'blk', axis=0, tiled=True)  283 us
    psum x1, waiting for transfers between devices, per_device(): gram = lax.psum(local_gram, ('blk', 'col'))  251 us
    dot_general x192, matrix products, tile_add(): return total + jnp.dot(weights, direction_rows, precision=highest)  238 us
    psum x3, blocking collectives, precondition(): lax.psum(jnp.sum(residual_now * scaled, axis=0), ('blk', 'col'))  226 us
    dot_general x197, matrix products, kernel_block(): lax.dot_general(left_rows, right_rows, (((1,), (1,)), ((), ())), preferre...  187 us
    psum x2, blocking collectives, per_device(): curvature = lax.psum(jnp.sum(direction_now * image, axis=0), ('blk', 'col'))  154 us
    all_gather x1, waiting for transfers between devices, per_device(): lax.all_gather(points.astype(jnp.float32), 'blk', axis=0, tiled=True)  116 us
  transfers between devices with their start and end apart: 10, of which 10 were waited for; matrix products, arithmetic and copies ran while one was open for 0% of the time, Pallas kernels for 0%

commit v1 on v0

--- a/solution.py
+++ b/solution.py
@@ -70,7 +70,7 @@
     local_gram = lax.dot_general(
         wide_factor, wide_factor, (((0,), (0,)), ((), ())), precision=highest
     )
-    gram = lax.psum(local_gram, ("blk", "col"))
+    gram = lax.psum(lax.psum(local_gram, "blk"), "col")
     gram = gram + noise_level * jnp.eye(2 * piv_count, dtype=jnp.float32)
     gram_chol = jnp.linalg.cholesky(gram)
 

time: 2440 us -> 3030 us (1.24)
  waiting for transfers between devices: 1180 us -> 1770 us
    psum x1 -> x2, waiting for transfers between devices: 251 us -> 734 us  [per_device(): gram = lax.psum(lax.psum(local_gram, 'blk'), 'col')]
    psum x2 -> x3, waiting for transfers between devices: 469 us -> 577 us  [precondition(): projection = lax.psum(local_proj, ('blk', 'col'))]
  transfers between devices with their start and end apart: 10 -> 12, of which waited for: 10 -> 12; matrix products, arithmetic and copies ran while one was open for 0% -> 5% of each run, Pallas kernels for 0% -> 0%
where the time goes in v1:
time: 3030 us; the launch traced here: 3000 us
  waiting for transfers between devices  1770 us (58%)
  blocking collectives  468 us (15%)
  matrix products  457 us (15%)
  other arithmetic  239 us (8%)
  local copies, waits for them, and re-layouts  35.8 us (1%)
    psum x2, waiting for transfers between devices, per_device(): gram = lax.psum(lax.psum(local_gram, 'blk'), 'col')  734 us
    psum x3, waiting for transfers between devices, precondition(): projection = lax.psum(local_proj, ('blk', 'col'))  577 us
    all_gather x3, waiting for transfers between devices, per_device(): lax.all_gather(direction_now, 'blk', axis=0, tiled=True)  294 us
    dot_general x192, matrix products, tile_add(): return total + jnp.dot(weights, direction_rows, precision=highest)  238 us
    psum x3, blocking collectives, precondition(): lax.psum(jnp.sum(residual_now * scaled, axis=0), ('blk', 'col'))  226 us
    dot_general x197, matrix products, kernel_block(): lax.dot_general(left_rows, right_rows, (((1,), (1,)), ((), ())), preferre...  187 us
    psum x2, blocking collectives, per_device(): curvature = lax.psum(jnp.sum(direction_now * image, axis=0), ('blk', 'col'))  154 us
    all_gather x1, waiting for transfers between devices, per_device(): lax.all_gather(points.astype(jnp.float32), 'blk', axis=0, tiled=True)  101 us
  transfers between devices with their start and end apart: 12, of which 12 were waited for; matrix products, arithmetic and copies ran while one was open for 5% of the time, Pallas kernels for 0%

profile of v1, /device:TPU:1, one launch (start us, length us, event | category | flops | bytes accessed | tf_op | source)
XLA Modules:
  0.0 3000.5 jit_solution(11560901591662236084)
XLA Ops:
  8.9 82.6 %all-reduce.19 = bf16[512,128]{1,0:T(8,128)(2,1)S(1)} all-reduce(f32[512,128]{1,0:T(8,128)S(1)} %fusion.57), channel_id=1, replica_groups=mesh['blk'=64,'col'=4] {'blk','col'}, use_global_device_ids=true, to_apply=%region_0.0 | all-reduce | flops 65536 | bytes 393216 | tf_op jit(solution)/shard_map/psum | solution.py:67
  92.1 11.7 cholesky.354
  103.9 9.8 custom-call.54
  114.3 11.7 cholesky.364
  129.2 4.4 while.53
  130.0 1.4 dynamic-slice.27
  132.1 1.4 dynamic-slice.27
  133.6 19.7 custom-call.55
  156.1 11.7 cholesky.381
  167.8 9.8 custom-call.56
  178.1 11.7 cholesky.391
  192.9 4.0 while.54
  193.5 1.4 bitcast_dynamic-update-slice_fusion.7
  195.5 1.4 bitcast_dynamic-update-slice_fusion.7
  196.9 19.7 custom-call.57
  218.0 2.0 fusion.240
  220.1 644.6 %all-reduce.10.cloned.1.call-done = f32[512,512]{1,0:T(8,128)} async-done(((f32[512,512]{1,0:T(8,128)}), f32[512,512]{1,0:T(8,128)}) %all-reduce.10.cloned.1.call-update) | async-done | bytes 1048592 | tf_op jit(solution)/shard_map/psum | solution.py:73
  866.5 89.6 %all-reduce.12.cloned.1.call-done = f32[512,512]{1,0:T(8,128)} async-done(((f32[512,512]{1,0:T(8,128)}), f32[512,512]{1,0:T(8,128)}) %all-reduce.12.cloned.1.call-update) | async-done | bytes 1048592 | tf_op jit(solution)/shard_map/psum | solution.py:73
  956.1 1.4 select_add_fusion
  958.1 11.7 cholesky.166
  970.0 9.8 custom-call.42
  980.5 11.7 cholesky.189
  993.6 9.9 custom-call.43
  1004.2 11.7 cholesky.292
  1016.6 9.8 custom-call.58
  1027.0 11.7 cholesky.305
  1042.3 10.8 while.55
  1043.0 2.0 bitcast_dynamic-update-slice_fusion.8
  1045.7 2.0 bitcast_dynamic-update-slice_fusion.8
  1048.4 2.0 bitcast_dynamic-update-slice_fusion.8
  1051.1 2.0 bitcast_dynamic-update-slice_fusion.8
  1053.1 40.1 %custom-call.59 = f32[4,128,128]{1,2,0:T(8,128)S(1)} custom-call(f32[4,128,128]{2,1,0:T(8,128)} %get-tuple-element.393), custom_call_target="InvertDiagBlocksLowerTriangular" | custom-call | tf_op jit(solution)/shard_map/jit(_cho_solve)/triangular_solve | solution.py:82
  1093.2 108.8 %all-reduce.14.cloned.1.call-done = f32[512,32]{0,1:T(8,128)} async-done(((f32[512,32]{0,1:T(8,128)}), f32[512,32]{0,1:T(8,128)}) %all-reduce.14.cloned.1.call-update) | async-done | bytes 65552 | tf_op jit(solution)/shard_map/psum | solution.py:81
  1209.1 5.2 all_gather.17
  1214.4 101.4 %all-gather.5.cloned.1.call-done = bf16[8192,128]{1,0:T(8,128)(2,1)} async-done(((bf16[128,128]{1,0:T(8,128)(2,1)}), bf16[8192,128]{1,0:T(8,128)(2,1)}) %all-gather.5.cloned.1.call-update) | async-done | bytes 2097168 | tf_op jit(solution)/shard_map/all_gather | solution.py:100
  1315.8 2.7 multiply_reduce_fusion
  1318.5 102.4 %all-gather.7.cloned.1.call-done = f32[8192,32]{0,1:T(8,128)} async-done(((f32[128,32]{0,1:T(8,128)}), f32[8192,32]{0,1:T(8,128)}) %all-gather.7.cloned.1.call-update) | async-done | bytes 1048592 | tf_op jit(solution)/shard_map/all_gather | solution.py:103
  1421.0 3.6 copy.29
  1424.5 144.7 %while.50 = (s32[]{:T(128)}, f32[512,32]{0,1:T(8,128)S(1)}, f32[512]{0:T(512)S(1)}, f32[64,128]{1,0:T(8,128)S(1)}, bf16[64,128,128]{2,1,0:T(8,128)(2,1)}, /*inde...) while((s32[]{:T(128)}, f32[512,32]{0,1:T(8,128)S(1)}, ...), condition=%wide.region_24.29_spmd.clone, body=%wide.region_23.28_spmd.clone.sunk | while | flops 42237952 | bytes 889451 | solution.py:115
  1430.0 1.2 convolution_add_fusion.6
  1439.1 1.2 convolution_add_fusion.6
  1443.6 1.2 convolution_add_fusion.6
  1448.1 1.2 convolution_add_fusion.6
  1457.2 1.2 convolution_add_fusion.6
  1461.7 1.2 convolution_add_fusion.6
  1475.3 1.2 convolution_add_fusion.6
  1479.8 1.2 convolution_add_fusion.6
  1569.9 21.1 reduce-scatter.4.cloned.1.call-done
  1591.8 77.0 %all-reduce.2 = (f32[32]{0:T(128)S(1)}, f32[32]{0:T(128)S(1)}) all-reduce(f32[32]{0:T(128)S(1)} %get-tuple-element.431, f32[32]{0:T(128)S(1)} %get-tuple-element.430), channel_id=1, replica_groups=mesh['blk'=64,'col'=4] {'blk','col'}, use_global_device_ids=true, to_apply=%region_20.25 | all-reduce | flops 64 | bytes 512 | tf_op jit(solution)/shard_map/psum | solution.py:86
  1670.0 234.3 %all-reduce.16.cloned.1.call-done = f32[512,32]{0,1:T(8,128)} async-done(((f32[512,32]{0,1:T(8,128)}), f32[512,32]{0,1:T(8,128)}) %all-reduce.16.cloned.1.call-update) | async-done | bytes 65552 | tf_op jit(solution)/shard_map/psum | solution.py:81
  1910.8 74.4 %psum.91 = f32[32]{0:T(128)S(1)} all-reduce(f32[32]{0:T(128)S(1)} %get-tuple-element.535), channel_id=1, replica_groups=mesh['blk'=64,'col'=4] {'blk','col'}, use_global_device_ids=true, to_apply=%region_30.35 | all-reduce | flops 32 | bytes 256 | tf_op jit(solution)/shard_map/psum | solution.py:86
  1986.0 95.6 %all-gather.9.cloned.1.call-done = f32[8192,32]{0,1:T(8,128)} async-done(((f32[128,32]{0,1:T(8,128)}), f32[8192,32]{0,1:T(8,128)}) %all-gather.9.cloned.1.call-update) | async-done | bytes 1048592 | tf_op jit(solution)/shard_map/all_gather | solution.py:103
  2081.6 3.6 copy.30
  2085.1 144.7 %while.51 = (s32[]{:T(128)}, f32[512,32]{0,1:T(8,128)S(1)}, f32[512]{0:T(512)S(1)}, f32[64,128]{1,0:T(8,128)S(1)}, bf16[64,128,128]{2,1,0:T(8,128)(2,1)}, /*inde...) while((s32[]{:T(128)}, f32[512,32]{0,1:T(8,128)S(1)}, ...), condition=%wide.region_32.37_spmd.clone, body=%wide.region_31.36_spmd.clone.sunk | while | flops 42237952 | bytes 889451 | solution.py:115
  2230.5 21.1 reduce-scatter.6.cloned.1.call-done
  2252.4 77.3 %psum.92 = f32[32]{0:T(128)S(1)} all-reduce(f32[32]{0:T(128)S(1)} %multiply_reduce_fusion.7), channel_id=1, replica_groups=mesh['blk'=64,'col'=4] {'blk','col'}, use_global_device_ids=true, to_apply=%region_35.40 | all-reduce | flops 32 | bytes 256 | tf_op jit(solution)/shard_map/psum | solution.py:120
  2331.6 234.3 %all-reduce.18.cloned.1.call-done = f32[512,32]{0,1:T(8,128)} async-done(((f32[512,32]{0,1:T(8,128)}), f32[512,32]{0,1:T(8,128)}) %all-reduce.18.cloned.1.call-update) | async-done | bytes 65552 | tf_op jit(solution)/shard_map/psum | solution.py:81
  2572.4 74.4 %psum.94 = f32[32]{0:T(128)S(1)} all-reduce(f32[32]{0:T(128)S(1)} %get-tuple-element.537), channel_id=1, replica_groups=mesh['blk'=64,'col'=4] {'blk','col'}, use_global_device_ids=true, to_apply=%region_38.43 | all-reduce | flops 32 | bytes 256 | tf_op jit(solution)/shard_map/psum | solution.py:86
  2647.6 95.6 %all-gather.11.cloned.1.call-done = f32[8192,32]{0,1:T(8,128)} async-done(((f32[128,32]{0,1:T(8,128)}), f32[8192,32]{0,1:T(8,128)}) %all-gather.11.cloned.1.call-update) | async-done | bytes 1048592 | tf_op jit(solution)/shard_map/all_gather | solution.py:103
  2743.2 3.6 copy.31
  2746.7 144.7 %while.52 = (s32[]{:T(128)}, f32[512,32]{0,1:T(8,128)S(1)}, f32[512]{0:T(512)S(1)}, f32[64,128]{1,0:T(8,128)S(1)}, bf16[64,128,128]{2,1,0:T(8,128)(2,1)}, /*inde...) while((s32[]{:T(128)}, f32[512,32]{0,1:T(8,128)S(1)}, ...), condition=%wide.region_40.45_spmd.clone, body=%wide.region_39.44_spmd.clone.sunk | while | flops 42237952 | bytes 889451 | solution.py:115
  2892.1 21.1 reduce-scatter.8.cloned.1.call-done
  2914.8 77.0 %psum.95 = f32[32]{0:T(128)S(1)} all-reduce(f32[32]{0:T(128)S(1)} %multiply_reduce_fusion.5), channel_id=1, replica_groups=mesh['blk'=64,'col'=4] {'blk','col'}, use_global_device_ids=true, to_apply=%region_43.48 | all-reduce | flops 32 | bytes 256 | tf_op jit(solution)/shard_map/psum | solution.py:120
  2991.8 1.4 multiply_subtract_fusion
  (771 shorter events, 469.3 us)
Async XLA Ops:
  7.2 119.0 %copy-start.5 = (bf16[128,128]{1,0:T(8,128)(2,1)S(1)}, bf16[128,128]{1,0:T(8,128)(2,1)}, u32[]{:S(2)}) copy-start(bf16[128,128]{1,0:T(8,128)(2,1)} %param.16) | copy-start | bytes 98308
  7.2 857.6 %all-reduce.10.cloned.1.call-start = ((), (), s32[]{:S(2)}) async-start(), calls=%async_computation.3 | async-start | bytes 2097152 | tf_op jit(solution)/shard_map/psum | solution.py:73
  156.0 708.8 %copy-start.8 = (f32[128,32]{0,1:T(8,128)S(1)}, f32[128,32]{0,1:T(8,128)}, u32[]{:S(2)}) copy-start(f32[128,32]{0,1:T(8,128)} %param.17) | copy-start | bytes 49156
  220.0 736.1 %all-reduce.12.cloned.1.call-start = ((), (), s32[]{:S(2)}) async-start(), calls=%async_computation.4 | async-start | bytes 2097152 | tf_op jit(solution)/shard_map/psum | solution.py:73
  864.8 337.3 %all-reduce.14.cloned.1.call-start = ((), (), s32[]{:S(2)}) async-start(), calls=%async_computation.5 | async-start | bytes 131072 | tf_op jit(solution)/shard_map/psum | solution.py:81
  865.9 449.9 %all-gather.5.cloned.1.call-start = ((), (), s32[]{:S(2)}) async-start(), calls=%async_computation.6 | async-start | bytes 2129920 | tf_op jit(solution)/shard_map/all_gather | solution.py:100
  866.4 554.5 %all-gather.7.cloned.1.call-start = ((), (), s32[]{:S(2)}) async-start(), calls=%async_computation.7 | async-start | bytes 1064960 | tf_op jit(solution)/shard_map/all_gather | solution.py:103
  956.1 1.8 copy-start
  980.2 229.0 %copy-start.6 = (bf16[128,128]{1,0:T(8,128)(2,1)S(1)}, bf16[128,128]{1,0:T(8,128)(2,1)}, u32[]{:S(2)}) copy-start(bf16[128,128]{1,0:T(8,128)(2,1)} %param.16) | copy-start | bytes 98308
  1209.0 381.9 %reduce-scatter.4.cloned.1.call-start = ((), (), s32[]{:S(2)}) async-start(), calls=%async_computation.8 | async-start | bytes 81920 | tf_op jit(solution)/shard_map/reduce_scatter | solution.py:117
  1569.2 0.6 copy-start.1
  1569.9 334.5 %all-reduce.16.cloned.1.call-start = ((), (), s32[]{:S(2)}) async-start(), calls=%async_computation.9 | async-start | bytes 131072 | tf_op jit(solution)/shard_map/psum | solution.py:81
  1670.0 411.6 %all-gather.9.cloned.1.call-start = ((), (), s32[]{:S(2)}) async-start(), calls=%async_computation.10 | async-start | bytes 1064960 | tf_op jit(solution)/shard_map/all_gather | solution.py:103
  1985.9 265.7 %reduce-scatter.6.cloned.1.call-start = ((), (), s32[]{:S(2)}) async-start(), calls=%async_computation.11 | async-start | bytes 81920 | tf_op jit(solution)/shard_map/reduce_scatter | solution.py:117
  1986.0 265.6 %copy-start.4 = (f32[128,32]{0,1:T(8,128)S(1)}, f32[128,32]{0,1:T(8,128)}, u32[]{:S(2)}) copy-start(f32[128,32]{0,1:T(8,128)} %multiply_add_fusion.4) | copy-start | bytes 49156
  2229.8 0.6 copy-start.2
  2230.5 335.5 %all-reduce.18.cloned.1.call-start = ((), (), s32[]{:S(2)}) async-start(), calls=%async_computation.12 | async-start | bytes 131072 | tf_op jit(solution)/shard_map/psum | solution.py:81
  2331.6 411.6 %all-gather.11.cloned.1.call-start = ((), (), s32[]{:S(2)}) async-start(), calls=%async_computation.13 | async-start | bytes 1064960 | tf_op jit(solution)/shard_map/all_gather | solution.py:103
  2647.5 265.7 %reduce-scatter.8.cloned.1.call-start = ((), (), s32[]{:S(2)}) async-start(), calls=%async_computation.14 | async-start | bytes 81920 | tf_op jit(solution)/shard_map/reduce_scatter | solution.py:117
  2647.6 265.6 %copy-start.7 = (f32[128,32]{0,1:T(8,128)S(1)}, f32[128,32]{0,1:T(8,128)}, u32[]{:S(2)}) copy-start(f32[128,32]{0,1:T(8,128)} %multiply_add_fusion.2) | copy-start | bytes 49156
  2891.4 0.6 copy-start.3
Sparse Core Ops, SparseCore 0:
  220.2 644.5 all-reduce.9
  867.6 88.4 all-reduce.11
  962.2 239.8 all-reduce.13
  1205.5 110.2 all-gather.4
  1319.7 101.2 all-gather.6
  1570.0 20.9 reduce-scatter.3
  1670.1 234.2 all-reduce.15
  1986.0 95.4 all-gather.8
  2230.6 20.9 reduce-scatter.5
  2331.7 234.2 all-reduce.17
  2647.6 95.4 all-gather.10
  2892.2 20.9 reduce-scatter.7
